TPU v7x, 512 devices: a whole 4x4x16 slice. The times are simulated.
512 devices in a mesh: dp: 32 (over y, x, core), tensor: 16 (over z).
Axes of the slice: x: 4, y: 4, z: 16, core: 2. Of those that a mesh axis runs over, the one named last changes fastest.
Arguments:
- hidden: bfloat16 [24576, 4096], P('dp', 'tensor'), may hold values from -4 to 4
- queries: bfloat16 [24576, 4096], P('dp', 'tensor')
- database: bfloat16 [1024, 128, 896], P('dp', 'tensor'), may hold values from -6 to 6
- w_key: bfloat16 [896, 4096], P(None, 'tensor'), may hold values from -0.1875 to 0.1875
- w_value: bfloat16 [896, 4096], P(None, 'tensor'), may hold values from -0.1875 to 0.1875
- w_out: bfloat16 [4096, 4096], P(None, 'tensor'), may hold values from -0.09375 to 0.09375
- owners: int32 [384, 2], P('dp'), may hold values from 0 to 31, all different within a row; in each aligned block of 12 rows (0 to 11, 12 to 23, ...) at most 2 rows name the same one
- entry_slots: int32 [384, 2], P('dp'), may hold values from 0 to 31
Outputs:
- mixed: bfloat16 [24576, 4096], P('dp', 'tensor')
Inputs may be any that keep to these rules, and one draw needn't show every extreme that they name: Among the spans of one dp index (aligned blocks of 12 rows) no owner is named more than 2 times, a bound that some block reaches; the 2 neighbours of a span have different owners.
All inputs are finite; a program needn't handle non-finite values.
Results may differ from a plain program's by a relative error of at most 0.012.
The roundings to bfloat16 on the way count: a program that leaves them out, or rounds other values in their place, can miss the bound.
Values may be sent and summed in bfloat16 or wider, within the bound.
A program may use at most 64 MiB of HBM per device.

v0:
```python
import math
import jax
import jax.numpy as jnp
from jax import lax
from jax.sharding import PartitionSpec as P

HEAD_DIM = 128


def per_device(hidden, queries, database, w_key, w_value, w_out, owners, entry_slots):
    dp_size = lax.axis_size("dp")
    span_count = owners.shape[0]
    per_span = owners.shape[1]
    capacity = max(2, (per_span * span_count + dp_size - 1) // dp_size)
    wanted = owners.reshape(-1)
    local_slot = entry_slots.reshape(-1)
    requests_here = wanted.shape[0]
    same_owner = wanted[:, None] == wanted[None, :]
    before = jnp.arange(requests_here)[None, :] < jnp.arange(requests_here)[:, None]
    order_in = jnp.sum(jnp.where(same_owner & before, 1, 0), axis=1).astype(jnp.int32)
    position = wanted * capacity + order_in
    placed = position[:, None] == jnp.arange(dp_size * capacity, dtype=jnp.int32)[None, :]
    request_table = jnp.sum(jnp.where(placed, (local_slot + 1)[:, None], 0), axis=0)
    request_table = request_table.reshape(dp_size, capacity)
    incoming = lax.all_to_all(request_table, "dp", split_axis=0, concat_axis=0, tiled=True)
    served_rows = jnp.maximum(incoming - 1, 0).reshape(-1)
    served = jnp.take(database, served_rows, axis=0)
    served = served.reshape(dp_size, capacity, database.shape[1], database.shape[2])
    replies = lax.all_to_all(served, "dp", split_axis=0, concat_axis=0, tiled=True)
    reply_rows = replies.reshape(dp_size * capacity, database.shape[1] * database.shape[2])
    fetched = jnp.dot(
        placed.astype(jnp.bfloat16), reply_rows, preferred_element_type=jnp.float32
    ).astype(jnp.bfloat16)
    fetched = fetched.reshape(requests_here, database.shape[1], database.shape[2])
    proj_weight = jnp.concatenate([w_key, w_value], axis=1)
    piece = lax.all_gather(fetched, "tensor", axis=1, tiled=True)
    flat_piece = piece.reshape(piece.shape[0] * piece.shape[1], piece.shape[2])
    result = jnp.dot(flat_piece, proj_weight, preferred_element_type=jnp.float32).astype(
        jnp.bfloat16
    )
    key_value = result.reshape(piece.shape[0], piece.shape[1], proj_weight.shape[1])
    width = w_key.shape[1]
    heads_here = width // HEAD_DIM
    key_value = key_value.reshape(
        span_count, per_span * key_value.shape[1], 2, heads_here, HEAD_DIM
    )
    key_rows = key_value[:, :, 0]
    value_rows = key_value[:, :, 1]
    span_size = queries.shape[0] // span_count
    query_rows = queries.reshape(span_count, span_size, heads_here, HEAD_DIM)
    score_scale = 1.0 / math.sqrt(HEAD_DIM)
    scores = (
        jnp.einsum("cihd,cjhd->chij", query_rows, key_rows, preferred_element_type=jnp.float32)
        * score_scale
    )
    row_max = jnp.max(scores, axis=-1, keepdims=True)
    weights = jnp.exp(scores - row_max)
    weights = weights / jnp.sum(weights, axis=-1, keepdims=True)
    softmax_low = weights.astype(jnp.bfloat16)
    attended = jnp.einsum(
        "chij,cjhd->cihd", softmax_low, value_rows, preferred_element_type=jnp.float32
    )
    attended = attended.astype(jnp.bfloat16).reshape(queries.shape[0], width)
    gathered = lax.all_gather(attended, "tensor", axis=1, tiled=True)
    projected = jnp.dot(gathered, w_out, preferred_element_type=jnp.float32)
    return (hidden.astype(jnp.float32) + projected).astype(jnp.bfloat16)


def solution(mesh):
    in_specs = (
        P("dp", "tensor"),
        P("dp", "tensor"),
        P("dp", "tensor", None),
        P(None, "tensor"),
        P(None, "tensor"),
        P(None, "tensor"),
        P("dp", None),
        P("dp", None),
    )
    out_specs = P("dp", "tensor")
    return jax.shard_map(
        per_device, mesh=mesh, in_specs=in_specs, out_specs=out_specs, check_vma=False
    )
```

profile of v0, /device:TPU:32, one launch (start us, length us, event | category | flops | bytes accessed | tf_op | source)
XLA Modules:
  0.0 276.5 jit_solution(5320684096094378514)
XLA Ops:
  6.5 0.9 copy.42
  7.5 0.1 reshape.77
  7.5 0.2 select_reduce_fusion.1
  7.7 0.7 broadcast_add_fusion
  8.4 0.1 copy.43
  8.5 0.1 add.43
  8.6 0.1 select_reduce_fusion
  8.7 0.1 all_to_all.9
  8.8 14.5 %all_to_all.14 = s32[32,1,2]{2,1,0:T(1,128)S(1)} all-to-all(s32[32,1,2]{2,1,0:T(1,128)S(1)} %bitcast.54), channel_id=1, replica_groups=mesh['dp'=32,'tensor'=16] {'dp'}, dimensions={0} | all-to-all | bytes 512 | tf_op jit(solution)/shard_map/all_to_all | solution.py:25
  23.3 0.1 copy.45
  23.4 0.1 copy.47
  23.5 0.1 reshape.85
  23.6 0.1 copy.46
  23.7 1.7 gather_fusion
  25.4 0.2 broadcast_select_fusion
  25.6 19.2 %all_to_all.15 = bf16[32,2,8,896]{3,2,1,0:T(8,128)(2,1)S(1)} all-to-all(bf16[32,2,8,896]{3,2,1,0:T(8,128)(2,1)S(1)} %broadcast_select_fusion), channel_id=1, replica_groups=mesh['dp'=32,'tensor'=16] {'dp'}, dimensions={0} | all-to-all | bytes 1835008 | tf_op jit(solution)/shard_map/all_to_all | solution.py:29
  44.8 0.1 copy.54
  45.0 0.3 convolution_convert_fusion
  45.3 0.8 copy.55
  46.2 0.1 reshape.81
  46.3 82.7 %all-gather.3.cloned.1.call-done = bf16[24,128,896]{2,1,0:T(8,128)(2,1)} async-done(((bf16[24,8,896]{2,1,0:T(8,128)(2,1)}), bf16[24,128,896]{2,1,0:T(8,128)(2,1)}) %all-gather.3.cloned.1.call-update) | async-done | bytes 5505040 | tf_op jit(solution)/shard_map/all_gather | solution.py:36
  128.9 7.7 %convolution_convert_fusion.1 = bf16[3072,512]{1,0:T(8,128)(2,1)} fusion(bf16[3072,896]{1,0:T(8,128)(2,1)} %bitcast.55, bf16[896,256]{1,0:T(8,128)(2,1)S(1)} %copy-done.3, bf16[896,256]{1,0:T(8,128)(2,1)} %param.11), kind=kOutput, calls=%fused_computation.3 | convolution fusion | flops 2821980160 | bytes 9568256 | tf_op jit(solution)/shard_map/dot_general | solution.py:38
  136.7 5.5 %reshape_reshape.3 = bf16[12,256,2,2,128]{4,3,2,1,0:T(2,128)(2,1)} reshape(bf16[3072,512]{1,0:T(8,128)(2,1)} %convolution_convert_fusion.1) | data formatting | bytes 6291456 | tf_op jit(solution)/shard_map/reshape;reshape | solution.py:44
  142.2 4.8 %fusion.25 = (bf16[12,256,1,2,128]{4,3,2,1,0:T(2,128)(2,1)S(1)}, bf16[12,256,1,2,128]{4,3,2,1,0:T(2,128)(2,1)}) fusion(bf16[12,256,2,2,128]{4,3,2,1,0:T(2,128)(2,1)} %reshape_reshape.3), kind=kLoop, calls=%fused_computation.38 | loop fusion | bytes 6291456 | tf_op jit(solution)/shard_map/slice | solution.py:47
  147.0 0.7 fusion.5
  147.7 1.1 copy-done.1
  148.9 0.5 fusion.26
  149.4 4.6 %fusion.11 = bf16[12,64,2,128]{3,1,2,0:T(8,128)(2,1)S(1)} fusion(bf16[12,256,1,2,128]{4,3,2,1,0:T(2,128)(2,1)} %get-tuple-element.6, f32[12,2,64]{2,1,0:T(2,128)S(1)} %fusion.26, f32[12,2,256,64]{2,3,1,0:T(8,128)} %copy-done.1), kind=kOutput, calls=%fused_computation.17 | convolution fusion | flops 102041344 | bytes 3545088 | tf_op jit(solution)/shard_map/chij,cjhd->cihd/dot_general | solution.py:60
  154.0 0.4 copy.51
  154.4 0.8 copy.70
  155.3 109.1 %all-gather.5.cloned.1.call-done = bf16[768,4096]{1,0:T(8,128)(2,1)} async-done(((bf16[768,256]{1,0:T(8,128)(2,1)}), bf16[768,4096]{1,0:T(8,128)(2,1)}) %all-gather.5.cloned.1.call-update) | async-done | bytes 6291472 | tf_op jit(solution)/shard_map/all_gather | solution.py:64
  264.3 5.3 %fusion.9 = bf16[768,256]{1,0:T(8,128)(2,1)} fusion(bf16[768,4096]{1,0:T(8,128)(2,1)} %all-gather.5.cloned.1.call-done, bf16[4096,256]{1,0:T(8,128)(2,1)S(1)} %copy-done, bf16[768,256]{1,0:T(8,128)(2,1)S(1)} %copy-done.4), kind=kOutput, calls=%fused_computation.15 | convolution fusion | flops 1611202560 | bytes 9175040 | tf_op jit(solution)/shard_map/dot_general | solution.py:65
  (17 shorter events, 0.1 us)
Async XLA Ops:
  6.5 257.8 %copy-start = (bf16[4096,256]{1,0:T(8,128)(2,1)S(1)}, bf16[4096,256]{1,0:T(8,128)(2,1)}, u32[]{:S(2)}) copy-start(bf16[4096,256]{1,0:T(8,128)(2,1)} %param.13) | copy-start | bytes 6291460
  6.5 122.4 %all-gather.3.cloned.1.call-start = ((), (), s32[]{:S(2)}) async-start(), calls=%async_computation.2 | async-start | bytes 5849088 | tf_op jit(solution)/shard_map/all_gather | solution.py:36
  45.0 1.2 copy-start.2
  45.0 83.9 %copy-start.3 = (bf16[896,256]{1,0:T(8,128)(2,1)S(1)}, bf16[896,256]{1,0:T(8,128)(2,1)}, u32[]{:S(2)}) copy-start(bf16[896,256]{1,0:T(8,128)(2,1)} %param.12) | copy-start | bytes 1376260
  46.1 218.2 %all-gather.5.cloned.1.call-start = ((), (), s32[]{:S(2)}) async-start(), calls=%async_computation.3 | async-start | bytes 6684672 | tf_op jit(solution)/shard_map/all_gather | solution.py:64
  147.7 1.2 copy-start.1
  154.0 110.3 %copy-start.4 = (bf16[768,256]{1,0:T(8,128)(2,1)S(1)}, bf16[768,256]{1,0:T(8,128)(2,1)}, u32[]{:S(2)}) copy-start(bf16[768,256]{1,0:T(8,128)(2,1)} %param.8) | copy-start | bytes 1179652
Sparse Core Ops, SparseCore 0:
  46.2 82.6 all-gather.2
  155.4 108.8 all-gather.4
where the time goes:
time: 277 us; the launch traced here: 276 us
  waiting for transfers between devices  192 us (69%)
  blocking collectives  33.7 us (12%)
  matrix products  18.7 us (7%)
  local copies, waits for them, and re-layouts  17.1 us (6%)
  between operations  13.5 us (5%)
    all_gather x1, waiting for transfers between devices, per_device(): gathered = lax.all_gather(attended, 'tensor', axis=1, tiled=True)  109 us
    all_gather x1, waiting for transfers between devices, per_device(): piece = lax.all_gather(fetched, 'tensor', axis=1, tiled=True)  82.7 us
    all_to_all x1, blocking collectives, per_device(): lax.all_to_all(served, 'dp', split_axis=0, concat_axis=0, tiled=True)  19.2 us
    all_to_all x1, blocking collectives, per_device(): lax.all_to_all(request_table, 'dp', split_axis=0, concat_axis=0, tiled=True)  14.5 us
    dot_general x1, matrix products, per_device(): jnp.dot(flat_piece, proj_weight, preferred_element_type=jnp.float32)  7.74 us
  transfers between devices with their start and end apart: 2, of which 2 were waited for; matrix products, arithmetic and copies ran while one was open for 0% of the time, Pallas kernels for 0%

commit v1 on v0

--- a/solution.py
+++ b/solution.py
@@ -61,7 +61,15 @@
         "chij,cjhd->cihd", softmax_low, value_rows, preferred_element_type=jnp.float32
     )
     attended = attended.astype(jnp.bfloat16).reshape(queries.shape[0], width)
-    gathered = lax.all_gather(attended, "tensor", axis=1, tiled=True)
+    gathered = jnp.concatenate(
+        jax.lax.all_to_all(
+            jnp.stack([attended] * jax.lax.axis_size("tensor")),
+            axis_name="tensor",
+            split_axis=0,
+            concat_axis=0,
+        ),
+        1,
+    )
     projected = jnp.dot(gathered, w_out, preferred_element_type=jnp.float32)
     return (hidden.astype(jnp.float32) + projected).astype(jnp.bfloat16)
 

time: 277 us -> 443 us (1.60)
  the two profiles are of different devices: /device:TPU:32 before, /device:TPU:2 now
where the time goes in v1:
time: 443 us; the launch traced here: 442 us
  blocking collectives  311 us (70%)
  waiting for transfers between devices  83.4 us (19%)
  local copies, waits for them, and re-layouts  17 us (4%)
  matrix products  15.9 us (4%)
  between operations  13.5 us (3%)
    all_to_all x1, blocking collectives, per_device(): jax.lax.all_to_all(jnp.stack([attended] * jax.lax.axis_size('tensor')), a...  277 us
    all_gather x1, waiting for transfers between devices, per_device(): piece = lax.all_gather(fetched, 'tensor', axis=1, tiled=True)  83.3 us
    all_to_all x1, blocking collectives, per_device(): lax.all_to_all(served, 'dp', split_axis=0, concat_axis=0, tiled=True)  19.2 us
    all_to_all x1, blocking collectives, per_device(): lax.all_to_all(request_table, 'dp', split_axis=0, concat_axis=0, tiled=True)  14.8 us
  transfers between devices with their start and end apart: 1, of which 1 were waited for; matrix products, arithmetic and copies ran while one was open for 0% of the time, Pallas kernels for 0%

profile of v1, /device:TPU:2, one launch (start us, length us, event | category | flops | bytes accessed | tf_op | source)
XLA Modules:
  0.0 442.4 jit_solution(14204347976980766215)
XLA Ops:
  6.5 0.8 broadcast_add_fusion
  7.4 0.1 copy.46
  7.5 0.1 add.43
  7.6 0.8 copy.45
  8.3 0.1 reshape.82
  8.4 0.2 select_reduce_fusion.1
  8.6 0.1 select_reduce_fusion
  8.7 0.1 all_to_all.12
  8.8 14.8 %all_to_all.19 = s32[32,1,2]{2,1,0:T(1,128)S(1)} all-to-all(s32[32,1,2]{2,1,0:T(1,128)S(1)} %bitcast.58), channel_id=1, replica_groups=mesh['dp'=32,'tensor'=16] {'dp'}, dimensions={0} | all-to-all | bytes 512 | tf_op jit(solution)/shard_map/all_to_all | solution.py:25
  23.7 0.1 copy.49
  23.8 0.1 copy.50
  23.9 0.1 reshape.91
  24.0 1.7 gather_fusion
  25.7 0.2 broadcast_select_fusion
  25.9 19.2 %all_to_all.20 = bf16[32,2,8,896]{3,2,1,0:T(8,128)(2,1)S(1)} all-to-all(bf16[32,2,8,896]{3,2,1,0:T(8,128)(2,1)S(1)} %broadcast_select_fusion), channel_id=1, replica_groups=mesh['dp'=32,'tensor'=16] {'dp'}, dimensions={0} | all-to-all | bytes 1835008 | tf_op jit(solution)/shard_map/all_to_all | solution.py:29
  45.1 0.1 copy.58
  45.3 0.3 convolution_convert_fusion
  45.6 0.8 copy.59
  46.4 0.1 reshape.86
  46.5 83.3 %all-gather.2.cloned.1.call-done = bf16[24,128,896]{2,1,0:T(8,128)(2,1)} async-done(((bf16[24,8,896]{2,1,0:T(8,128)(2,1)}), bf16[24,128,896]{2,1,0:T(8,128)(2,1)}) %all-gather.2.cloned.1.call-update) | async-done | bytes 5505040 | tf_op jit(solution)/shard_map/all_gather | solution.py:36
  129.9 7.7 %convolution_convert_fusion.1 = bf16[3072,512]{1,0:T(8,128)(2,1)} fusion(bf16[3072,896]{1,0:T(8,128)(2,1)} %bitcast.59, bf16[896,256]{1,0:T(8,128)(2,1)S(1)} %copy-done.4, bf16[896,256]{1,0:T(8,128)(2,1)} %param.11), kind=kOutput, calls=%fused_computation.3 | convolution fusion | flops 2821980160 | bytes 9568256 | tf_op jit(solution)/shard_map/dot_general | solution.py:38
  137.6 5.5 %reshape_reshape.3 = bf16[12,256,2,2,128]{4,3,2,1,0:T(2,128)(2,1)} reshape(bf16[3072,512]{1,0:T(8,128)(2,1)} %convolution_convert_fusion.1) | data formatting | bytes 6291456 | tf_op jit(solution)/shard_map/reshape;reshape | solution.py:44
  143.1 4.8 %fusion.25 = (bf16[12,256,1,2,128]{4,3,2,1,0:T(2,128)(2,1)S(1)}, bf16[12,256,1,2,128]{4,3,2,1,0:T(2,128)(2,1)}) fusion(bf16[12,256,2,2,128]{4,3,2,1,0:T(2,128)(2,1)} %reshape_reshape.3), kind=kLoop, calls=%fused_computation.38 | loop fusion | bytes 6291456 | tf_op jit(solution)/shard_map/slice | solution.py:47
  148.0 0.7 fusion.5
  148.7 1.1 copy-done.1
  149.8 0.5 fusion.26
  150.3 4.6 %fusion.11 = bf16[12,64,2,128]{3,1,2,0:T(8,128)(2,1)S(1)} fusion(bf16[12,256,1,2,128]{4,3,2,1,0:T(2,128)(2,1)} %get-tuple-element.6, f32[12,2,64]{2,1,0:T(2,128)S(1)} %fusion.26, f32[12,2,256,64]{2,3,1,0:T(8,128)} %copy-done.1), kind=kOutput, calls=%fused_computation.17 | convolution fusion | flops 102041344 | bytes 3545088 | tf_op jit(solution)/shard_map/chij,cjhd->cihd/dot_general | solution.py:60
  155.0 0.4 copy.54
  155.4 0.2 copy.55
  155.6 0.6 stack.3
  156.3 276.8 %all_to_all.21 = bf16[16,768,256]{1,2,0:T(8,128)(2,1)S(1)} all-to-all(bf16[16,768,256]{1,2,0:T(8,128)(2,1)S(1)} %stack.3), channel_id=1, replica_groups=mesh['dp'=32,'tensor'=16] {'tensor'}, dimensions={0} | all-to-all | bytes 12582912 | tf_op jit(solution)/shard_map/all_to_all | solution.py:65
  433.0 2.6 fusion.9
  (17 shorter events, 0.2 us)
Async XLA Ops:
  6.5 426.5 %copy-start = (bf16[4096,256]{1,0:T(8,128)(2,1)S(1)}, bf16[4096,256]{1,0:T(8,128)(2,1)}, u32[]{:S(2)}) copy-start(bf16[4096,256]{1,0:T(8,128)(2,1)} %param.13) | copy-start | bytes 6291460
  6.5 123.3 %all-gather.2.cloned.1.call-start = ((), (), s32[]{:S(2)}) async-start(), calls=%async_computation.3 | async-start | bytes 5849088 | tf_op jit(solution)/shard_map/all_gather | solution.py:36
  45.3 1.1 copy-start.3
  45.3 84.6 %copy-start.4 = (bf16[896,256]{1,0:T(8,128)(2,1)S(1)}, bf16[896,256]{1,0:T(8,128)(2,1)}, u32[]{:S(2)}) copy-start(bf16[896,256]{1,0:T(8,128)(2,1)} %param.12) | copy-start | bytes 1376260
  148.7 1.2 copy-start.1
  156.2 276.8 %copy-start.2 = (bf16[768,256]{1,0:T(8,128)(2,1)S(1)}, bf16[768,256]{1,0:T(8,128)(2,1)}, u32[]{:S(2)}) copy-start(bf16[768,256]{1,0:T(8,128)(2,1)} %param.8) | copy-start | bytes 1179652
Sparse Core Ops, SparseCore 0:
  46.5 83.2 all-gather.1
